TPU v7x, 32 devices: a whole 2x2x4 slice. The times are simulated.
32 devices in a mesh: gx: 4 (over z), gy: 8 (over y, x, core).
Axes of the slice: x: 2, y: 2, z: 4, core: 2. Of those that a mesh axis runs over, the one named last changes fastest.
Arguments:
- displacement: float32 [3, 128, 5, 1024], P(None, 'gx', None, 'gy'), may hold values from -5 to 5
- velocity: float32 [3, 128, 5, 1024], P(None, 'gx', None, 'gy'), may hold values from -4 to 4
- stiffness: float32 [128, 5, 1024], P('gx', None, 'gy'), may hold values from 0.5 to 2
- inverse_mass: float32 [128, 5, 1024], P('gx', None, 'gy'), may hold values from 0.5 to 2
- facing: int32 [128, 8, 8], P('gx', 'gy'), may hold values from 0 to 1023, as said below
Outputs:
- final_displacement: float32 [3, 128, 5, 1024], P(None, 'gx', None, 'gy')
- final_velocity: float32 [3, 128, 5, 1024], P(None, 'gx', None, 'gy')
Inputs may be any that keep to these rules, and one draw needn't show every extreme that they name: facing[x, j, k] names block x' * 8 + j'. For each aligned run of 32 rows x and each j, the 256 entries name blocks with each pair (x' // 32, j') exactly 8 times; repeats are allowed.
All inputs are finite; a program needn't handle non-finite values.
Results may differ from a plain program's by a relative error of at most 0.0001.
Values sent between devices are 32-bit elements; how exact they have to be, the bound alone decides.
A program may use at most 64 MiB of HBM per device.

v0:
```python
import functools
import math
import jax
import jax.numpy as jnp
from jax import lax
from jax.experimental import pallas as pl
from jax.experimental.pallas import tpu as pltpu
from jax.sharding import PartitionSpec as P

STEPS = 2

time_step = 0.2
penalty = 4.0
damping = 1.0
kernel_width = 4.0
frame_extent = 4.0

bf16 = jnp.bfloat16
f32 = jnp.float32


def internal_force(padded_disp, padded_stiff, displacement):
    size_x, size_z, size_y = displacement.shape[1:]
    s = padded_disp[:, 1:] + padded_disp[:, :-1]
    s = s[:, :, 1:] + s[:, :, :-1]
    s = s[:, :, :, 1:] + s[:, :, :, :-1]
    stiff = padded_stiff[: size_x + 1, : size_z + 1, : size_y + 1]
    w = jnp.concatenate([stiff[None] * (s * 0.125), stiff[None]], axis=0)
    w = w[:, 1:] + w[:, :-1]
    w = w[:, :, 1:] + w[:, :, :-1]
    w = w[:, :, :, 1:] + w[:, :, :, :-1]
    return w[:3] - displacement * w[3:]


def split3(x):
    a = x.astype(bf16).astype(f32)
    r = x - a
    b = r.astype(bf16).astype(f32)
    return a, b, r - b


def far_parts(x):
    a, b, c = split3(x)
    rhs = jnp.concatenate([a, b, a, b, c, a], axis=0).astype(bf16)
    lhs = jnp.concatenate([a, b, c, jnp.zeros_like(a)], axis=0).astype(bf16)
    return rhs, lhs


def contact_kernel(rev_row, rev_src, fwd, own_ref, all_ref, out_ref, own_t, acc):
    rows, width = own_ref.shape[0] // 8, own_ref.shape[1]
    row_id = lax.broadcasted_iota(jnp.int32, (8, width), 0)

    @pl.loop(0, rows)
    def _(r):
        x = own_ref[pl.ds(pl.multiple_of(r * 8, 8), 8), :]
        norm = jnp.broadcast_to(x[3:4], x.shape)
        y = jnp.where(row_id < 3, 2.0 * x, jnp.where(row_id == 3, 1.0, jnp.where(row_id == 4, norm, 0.0)))
        a, b, c = split3(y)
        pack = jnp.concatenate([a, a, b, b, a, c], axis=0)
        own_t[r] = pack.T.astype(bf16)

    def pairs(r, blocks):
        parts = [far_parts(all_ref[pl.ds(pl.multiple_of(b * 8, 8), 8), :]) for b in blocks]
        far = jnp.concatenate([p[0] for p in parts], axis=1)
        lhs = jnp.concatenate([p[1] for p in parts], axis=1)
        e = jnp.dot(own_t[r], far, preferred_element_type=f32)
        w = jnp.exp2(e)
        hi = w.astype(bf16)
        dims = (((1,), (1,)), ((), ()))
        t = lax.dot_general(hi, lhs, dims, preferred_element_type=f32).T
        return t[0:8] + t[8:16] + t[16:24]

    per_row = fwd.shape[0] // rows

    @pl.loop(0, rows, unroll=8)
    def _(r):
        t = pairs(r, [fwd[r * per_row + k] for k in range(per_row)])
        acc[r] = t

    unroll = 32

    @pl.loop(0, rev_row.shape[0] // unroll)
    def _(g):
        got = []
        for k in range(unroll):
            r = rev_row[g * unroll + k]
            got.append((r, pairs(r, [rev_src[g * unroll + k]])))
        for r, t in got:
            acc[r] = acc[r] + t

    @pl.loop(0, rows)
    def _(r):
        x = own_ref[pl.ds(pl.multiple_of(r * 8, 8), 8), :]
        t = acc[r]
        out_ref[r] = x * t[4:5] - t


def contact_call(rev_row, rev_src, fwd, own, everyone):
    rows, width = own.shape[0] // 8, own.shape[1]
    smem = pl.BlockSpec(memory_space=pltpu.SMEM)
    vmem = pl.BlockSpec(memory_space=pltpu.VMEM)
    return pl.pallas_call(
        contact_kernel,
        out_shape=jax.ShapeDtypeStruct((rows, 8, width), f32),
        in_specs=[smem, smem, smem, vmem, vmem],
        out_specs=vmem,
        scratch_shapes=[
            pltpu.VMEM((rows, width, 48), bf16),
            pltpu.VMEM((rows, 8, width), f32),
        ],
        name="contact",
    )(rev_row, rev_src, fwd, own, everyone)


def edge_pieces(columns):
    tall = -(-columns // 8) * 8
    pieces = []
    start = 0
    for dx in (-1, 0, 1):
        for dy in (-1, 0, 1):
            if (dx, dy) != (0, 0):
                rows = tall if dy == 0 else 8
                pieces.append((dx, dy, start, rows))
                start += rows
    return pieces, start


def gather_kernel(count_gx, count_gy, pieces, own, edges, out, halo, local_sem, send_sems, recv_sems, edge_send, edge_recv):
    gx = lax.axis_index("gx")
    gy = lax.axis_index("gy")
    bits = count_gy.bit_length() - 1
    flips = [(1 - 2 * ((gy // (1 << k)) % 2)) * (1 << k) for k in range(bits)]
    side = gy % 2
    middle = list(range(1, bits))
    steps = [side * flips[b] + (1 - side) * flips[a] for a, b in zip(middle, middle[::-1])]
    steps.append(flips[0])

    peers = [(lax.rem(gx + k, count_gx), gy) for k in range(1, count_gx)]
    peers += [(gx, gy + step) for step in steps]
    around = [
        (lax.rem(gx + dx + count_gx, count_gx), lax.rem(gy + dy + count_gy, count_gy))
        for dx, dy, _, _ in pieces
    ]
    barrier = pltpu.get_barrier_semaphore()
    for peer in peers + around:
        pl.semaphore_signal(barrier, inc=1, device_id=peer, device_id_type=pl.DeviceIdType.MESH)
    pl.semaphore_wait(barrier, len(peers) + len(around))

    here = gx * count_gy + gy
    keep = pltpu.make_async_copy(own, out.at[here], local_sem)
    keep.start()
    started = []

    def send(slot, peer):
        copy = pltpu.make_async_remote_copy(
            src_ref=own if slot is None else out.at[slot],
            dst_ref=out.at[here if slot is None else slot],
            send_sem=send_sems.at[len(started)],
            recv_sem=recv_sems.at[here if slot is None else slot],
            device_id=peer,
            device_id_type=pl.DeviceIdType.MESH,
        )
        copy.start()
        started.append(copy)

    def arrived(slot):
        pltpu.make_async_remote_copy(
            src_ref=own,
            dst_ref=out.at[slot],
            send_sem=send_sems.at[0],
            recv_sem=recv_sems.at[slot],
            device_id=peers[0],
            device_id_type=pl.DeviceIdType.MESH,
        ).wait_recv()

    for peer in peers:
        send(None, peer)
    edge_copies = []
    for n, (dx, dy, start, rows) in enumerate(pieces):
        copy = pltpu.make_async_remote_copy(
            src_ref=edges.at[pl.ds(start, rows)],
            dst_ref=halo.at[pl.ds(start, rows)],
            send_sem=edge_send.at[n],
            recv_sem=edge_recv.at[n],
            device_id=around[n],
            device_id_type=pl.DeviceIdType.MESH,
        )
        copy.start()
        edge_copies.append(copy)
    half = 1 << (bits - 1)
    waves = [(k, m) for total in range(count_gx + half - 1) for m in range(half)
             for k in [total - m] if 0 <= k < count_gx and (k, m) != (0, 0)]
    for k, m in waves:
        column = gy
        for b in range(bits - 1):
            if m >> b & 1:
                column = column + steps[b]
        slot = lax.rem(gx + k, count_gx) * count_gy + column
        arrived(slot)
        for b in range(m.bit_length(), bits):
            send(slot, (gx, gy + steps[b]))
    for k, m in [(0, 0)] + waves:
        column = gy + flips[0]
        for b in range(bits - 1):
            if m >> b & 1:
                column = column + steps[bits - 2 - b]
        arrived(lax.rem(gx + k, count_gx) * count_gy + column)
    keep.wait()
    for copy in edge_copies:
        copy.wait()
    for copy in started:
        copy.wait_send()


def gather_call(own, edges, pieces, count_gx, count_gy):
    devices_all = count_gx * count_gy
    bits = count_gy.bit_length() - 1
    half = count_gy // 2
    sends = count_gx - 1 + bits
    for m in range(half):
        sends += (count_gx - (m == 0)) * (bits - m.bit_length())
    return pl.pallas_call(
        functools.partial(gather_kernel, count_gx, count_gy, pieces),
        out_shape=(
            jax.ShapeDtypeStruct((devices_all,) + own.shape, f32),
            jax.ShapeDtypeStruct(edges.shape, f32),
        ),
        in_specs=[pl.BlockSpec(memory_space=pltpu.VMEM)] * 2,
        out_specs=(pl.BlockSpec(memory_space=pl.ANY), pl.BlockSpec(memory_space=pl.ANY)),
        scratch_shapes=[
            pltpu.SemaphoreType.DMA,
            pltpu.SemaphoreType.DMA((sends,)),
            pltpu.SemaphoreType.DMA((devices_all,)),
            pltpu.SemaphoreType.DMA((len(pieces),)),
            pltpu.SemaphoreType.DMA((len(pieces),)),
        ],
        compiler_params=pltpu.CompilerParams(collective_id=0, has_side_effects=True),
        name="gather",
    )(own, edges)


def pack_edges(stacked, pieces):
    fields, width_x, depth, width_y = stacked.shape
    columns = fields * depth
    sides_y = {-1: stacked[:, :, :, 0], 1: stacked[:, :, :, width_y - 1]}
    parts = []
    for dx, dy, _, rows in pieces:
        x = 0 if dx < 0 else width_x - 1
        if dy == 0:
            part = stacked[:, x].reshape(columns, width_y)
            part = jnp.pad(part, ((0, rows - columns), (0, 0)))
        else:
            part = sides_y[dy] if dx == 0 else sides_y[dy][:, x]
            part = part.reshape(-1)
            part = jnp.pad(part, (0, rows * width_y - part.shape[0])).reshape(rows, width_y)
        parts.append(part)
    return jnp.concatenate(parts, axis=0)


def unpack_edges(halo, stacked, pieces):
    fields, width_x, depth, width_y = stacked.shape
    columns = fields * depth
    got = {}
    for dx, dy, start, rows in pieces:
        part = halo[start : start + rows]
        if dy == 0:
            part = part[:columns].reshape(fields, 1, depth, width_y)
        else:
            tall = width_x if dx == 0 else 1
            part = part.reshape(-1)[: columns * tall].reshape(fields, tall, depth, 1)
        got[-dx, -dy] = part
    got[0, 0] = stacked
    lines = [jnp.concatenate([got[dx, dy] for dx in (-1, 0, 1)], axis=1) for dy in (-1, 0, 1)]
    return jnp.concatenate(lines, axis=3)


def local(displacement, velocity, stiffness, inverse_mass, facing):
    count_gx = lax.axis_size("gx")
    count_gy = lax.axis_size("gy")
    devices_all = count_gx * count_gy
    width_x, depth, width_y = stiffness.shape
    global_x = lax.axis_index("gx") * width_x + jnp.arange(width_x, dtype=jnp.int32)
    global_y = lax.axis_index("gy") * width_y + jnp.arange(width_y, dtype=jnp.int32)
    layer_index = jnp.arange(depth, dtype=jnp.int32)
    inside = (
        (global_x < width_x * count_gx - 1)[:, None, None]
        & (layer_index < depth - 1)[None, :, None]
        & (global_y < width_y * count_gy - 1)[None, None, :]
    )
    masked_stiff = jnp.where(inside, stiffness, 0.0)
    per_row = facing.shape[2]
    requests = per_row * width_x
    capacity = requests // devices_all
    me = lax.axis_index("gx") * count_gy + lax.axis_index("gy")
    wanted = facing.reshape(requests)
    extra = -(-requests // (8 * width_y))
    unit = width_x + extra
    wanted_x = wanted // count_gy
    fwd = (wanted_x // width_x * count_gy + wanted % count_gy) * unit + wanted_x % width_x
    place = (jnp.arange(width_y, dtype=f32) - (width_y - 1) / 2.0) * (frame_extent / width_y)
    frame = jnp.stack([jnp.zeros_like(place), place, jnp.zeros_like(place)], axis=0)[:, None, :]
    scale = math.sqrt(math.log2(math.e) / kernel_width)
    stiff_coef = penalty / (8.0 * width_y)
    damp_coef = damping / (8.0 * width_y)

    pieces, _ = edge_pieces(4 * depth)

    for repeat in range(STEPS):
        p = displacement[:, :, depth - 1, :] + frame
        q = stiff_coef * p - damp_coef * velocity[:, :, depth - 1, :]
        sp = scale * p
        norm = -jnp.sum(sp * sp, axis=0, keepdims=True)
        surface = jnp.concatenate([sp, norm, jnp.ones_like(norm), q], axis=0).transpose(1, 0, 2)
        surface = surface.reshape(width_x * 8, width_y)
        tail = jnp.pad(fwd.astype(f32), (0, extra * 8 * width_y - requests)).reshape(extra * 8, width_y)
        stacked = jnp.concatenate([displacement, masked_stiff[None]], axis=0)
        edges = pack_edges(stacked, pieces)
        everyone, halo = gather_call(
            jnp.concatenate([surface, tail], axis=0), edges, pieces, count_gx, count_gy
        )
        if repeat == 0:
            table = everyone[:, width_x * 8 :].reshape(devices_all, -1)[:, :requests].astype(jnp.int32)
            mine = table // unit == me
            ordinal = jnp.arange(requests, dtype=jnp.int32)
            upto = (ordinal[:, None] <= ordinal[None, :]).astype(bf16)
            rank = jnp.dot(mine.astype(bf16), upto, preferred_element_type=f32)
            slot = (jnp.arange(capacity, dtype=jnp.int32) + 1).astype(f32)
            pick = mine[:, None, :] & (rank[:, None, :] == slot[None, :, None])
            rev_row = jnp.sum(jnp.where(pick, (table % unit)[:, None, :], 0), axis=2).reshape(requests)
            source = jnp.arange(devices_all, dtype=jnp.int32)[:, None] * unit + (ordinal // per_row)[None, :]
            rev_src = jnp.sum(jnp.where(pick, source[:, None, :], 0), axis=2).reshape(requests)
        everyone = everyone.reshape(-1, width_y)
        padded = unpack_edges(halo, stacked, pieces)
        padded = jnp.pad(padded, ((0, 0), (0, 0), (1, 1), (0, 0)))
        internal = internal_force(padded[:3], padded[3], displacement)
        contact = contact_call(rev_row, rev_src, fwd, surface, everyone)
        contact = contact[:, 5:8, :].transpose(1, 0, 2)
        total_force = internal.at[:, :, depth - 1, :].add(contact)
        velocity = velocity + time_step * inverse_mass[None] * total_force
        displacement = displacement + time_step * velocity
    return (displacement, velocity)


def solution(mesh):
    in_specs = (
        P(None, "gx", None, "gy"),
        P(None, "gx", None, "gy"),
        P("gx", None, "gy"),
        P("gx", None, "gy"),
        P("gx", "gy", None),
    )
    out_specs = (P(None, "gx", None, "gy"), P(None, "gx", None, "gy"))
    return jax.shard_map(local, mesh=mesh, in_specs=in_specs, out_specs=out_specs, check_vma=False)
```

profile of v0, /device:TPU:8, one launch (start us, length us, event | category | flops | bytes accessed | tf_op | source)
XLA Modules:
  0.0 151.8 jit_solution(7830254722988014210)
XLA Ops:
  0.9 0.8 copy.141
  2.3 1.0 fusion.52
  3.3 0.9 fusion.33
  4.3 1.0 and_select_fusion
  5.2 0.9 broadcast_multiply_fusion.2
  6.1 0.8 multiply_reduce_fusion.1
  8.2 0.9 copy.147
  9.5 0.9 copy.146
  12.2 37.4 %gather.2 = (f32[32,264,128]{2,1,0:T(8,128)}, f32[96,128]{1,0:T(8,128)}) custom-call(f32[264,128]{1,0:T(8,128)} %pad_maximum_fusion.3.own, f32[96,128]{1,0:T(8,128)} %copy-done.5), custom_call_target="tpu_custom_call" | custom-call | tf_op jit(solution)/shard_map/gather/pallas_call | solution.py:222
  51.0 0.7 fusion.46
  52.6 0.9 slice.359
  53.9 1.2 select_reduce_fusion
  56.4 19.4 %contact.2 = f32[32,8,128]{2,1,0:T(8,128)} custom-call(s32[256]{0:T(256)} %reshape.377.rev_row, s32[256]{0:T(256)} %reshape.378.rev_src, s32[256]{0:T(256)} %get-tuple-element.57.fwd, f32[256,128]{1,0:T(8,128)} %bitcast.177, f32[8448,128]{1,0:T(8,128)} %bitcast.171), custom_call_target="tpu_custom_call" | custom-call | tf_op jit(solution)/shard_map/contact/pallas_call | solution.py:102
  75.8 0.9 slice.430
  76.7 1.0 copy.154
  77.7 1.0 copy.151
  83.0 0.9 copy.169
  84.2 0.9 copy.168
  87.0 35.3 %gather.3 = (f32[32,264,128]{2,1,0:T(8,128)}, f32[96,128]{1,0:T(8,128)}) custom-call(f32[264,128]{1,0:T(8,128)} %pad_maximum_fusion.2.own, f32[96,128]{1,0:T(8,128)} %copy-done.6), custom_call_target="tpu_custom_call" | custom-call | tf_op jit(solution)/shard_map/gather/pallas_call | solution.py:222
  122.3 19.2 %contact.3 = f32[32,8,128]{2,1,0:T(8,128)} custom-call(s32[256]{0:T(256)} %reshape.377.rev_row, s32[256]{0:T(256)} %reshape.378.rev_src, s32[256]{0:T(256)} %get-tuple-element.57.fwd, f32[256,128]{1,0:T(8,128)} %bitcast.179, f32[8448,128]{1,0:T(8,128)} %bitcast.172), custom_call_target="tpu_custom_call" | custom-call | tf_op jit(solution)/shard_map/contact/pallas_call | solution.py:102
  142.7 1.1 copy.179
  143.8 1.1 copy.174
  144.9 2.2 %fusion.3 = f32[4,34,7,130]{3,0,1,2:T(4,128)S(1)} fusion(f32[4,1,5,1]{3,0,1,2:T(4,128)S(1)} %copy.180, f32[4,32,5,1]{3,0,1,2:T(4,128)S(1)} %copy.179, f32[4,1,5,1]{3,0,1,2:T(4,128)S(1)} %copy.178, f32[4,1,5,128]{3,0,1,2:T(4,128)S(1)} %copy.177, f32[4,1,5,1]{3,0,1,2:T(4,128)S(1)} %copy.175, f32[4,1,5,128]{3,0,1,2:T(4,128)S(1)} %copy.176, ...), kind=kLoop, calls=%fused_computation.17 | loop fusion | flops 2722720 | bytes 848640 | tf_op jit(solution)/shard_map/concatenate | solution.py:274
  150.3 0.7 copy.186
  (163 shorter events, 19.3 us)
Async XLA Ops:
  0.6 7.2 %copy-start = (f32[3,32,5,128]{3,1,2,0:T(8,128)S(1)}, f32[3,32,5,128]{3,1,2,0:T(8,128)}, u32[]{:S(2)}) copy-start(f32[3,32,5,128]{3,1,2,0:T(8,128)} %param.9) | copy-start | bytes 737284
  7.2 2.3 %copy-start.1 = (f32[32,8,128]{2,1,0:T(8,128)}, f32[32,8,128]{2,1,0:T(8,128)S(1)}, u32[]{:S(2)}) copy-start(f32[32,8,128]{2,1,0:T(8,128)S(1)} %copy.219) | copy-start | bytes 393220
  11.6 0.6 copy-start.5
  80.0 0.9 copy-start.3
  81.6 2.6 %copy-start.2 = (f32[32,8,128]{2,1,0:T(8,128)}, f32[32,8,128]{2,1,0:T(8,128)S(1)}, u32[]{:S(2)}) copy-start(f32[32,8,128]{2,1,0:T(8,128)S(1)} %copy.218) | copy-start | bytes 393220
  86.4 0.6 copy-start.6
  122.3 19.2 %copy-start.7 = (f32[96,128]{1,0:T(8,128)S(1)}, f32[96,128]{1,0:T(8,128)}, u32[]{:S(2)}) copy-start(f32[96,128]{1,0:T(8,128)} %get-tuple-element.32) | copy-start | bytes 147460
  149.1 0.9 copy-start.4
where the time goes:
time: 153 us; the launch traced here: 152 us
  Pallas kernels  111 us (73%)
  local copies, waits for them, and re-layouts  24 us (16%)
  other arithmetic  15 us (10%)
    pallas_call x2, Pallas kernels, gather_call(): pl.pallas_call(functools.partial(gather_kernel, count_gx, count_gy, piece...  72.6 us
    pallas_call x2, Pallas kernels, contact_call(): pl.pallas_call(contact_kernel, out_shape=jax.ShapeDtypeStruct((rows, 8, w...  38.6 us
    reshape x22, local copies, waits for them, and re-layouts, unpack_edges(): part = part.reshape(-1)[:columns * tall].reshape(fields, tall, depth, 1)  6.87 us
    unnamed x34, local copies, waits for them, and re-layouts  4.67 us
    slice x8, local copies, waits for them, and re-layouts, pack_edges(): sides_y = {-1: stacked[:, :, :, 0], 1: stacked[:, :, :, width_y - 1]}  4.23 us

commit v1 on v0

v1 whole, which is shorter than its diff:
```python
import functools
import math
import jax
import jax.numpy as jnp
from jax import lax
from jax.experimental import pallas as pl
from jax.experimental.pallas import tpu as pltpu
from jax.sharding import PartitionSpec as P

STEPS = 2

time_step = 0.2
penalty = 4.0
damping = 1.0
kernel_width = 4.0
frame_extent = 4.0

bf16 = jnp.bfloat16
f32 = jnp.float32
i32 = jnp.int32
MESH = pl.DeviceIdType.MESH
AHEAD = 2
PACK = 256


def split3(x):
    a = x.astype(bf16).astype(f32)
    r = x - a
    b = r.astype(bf16).astype(f32)
    return a, b, r - b


def table_kernel(count_gy, capacity, per_row, width_x, wanted_ref, out_ref):
    devices = out_ref.shape[0]
    requests = wanted_ref.shape[1]
    wanted = wanted_ref[...]
    wanted_x = wanted // count_gy
    device = wanted_x // width_x * count_gy + wanted % count_gy
    far = (wanted_x % width_x).astype(f32)
    own = (lax.broadcasted_iota(i32, (1, requests), 1) // per_row).astype(f32)
    mine = lax.broadcasted_iota(i32, (devices, requests), 0) == device
    mine_f = jnp.where(mine, 1.0, 0.0)
    upto = jnp.where(
        lax.broadcasted_iota(i32, (requests, requests), 0) <= lax.broadcasted_iota(i32, (requests, requests), 1), 1.0, 0.0
    ).astype(bf16)
    rank = jnp.dot(mine_f.astype(bf16), upto, preferred_element_type=f32)
    place = jnp.sum(mine_f * rank, axis=0, keepdims=True).astype(i32)
    at = jnp.where(lax.broadcasted_iota(i32, (128, requests), 0) + 1 == place, 1.0, 0.0).astype(bf16)
    dims = (((1,), (1,)), ((), ()))
    own_table = lax.dot_general((mine_f * own).astype(bf16), at, dims, preferred_element_type=f32)
    far_table = lax.dot_general((mine_f * far).astype(bf16), at, dims, preferred_element_type=f32)
    table = own_table.astype(i32) * PACK + far_table.astype(i32)
    for d in range(devices):
        out_ref[d] = table[d : d + 1]


def step_kernel(count_gx, count_gy, capacity, disp_ref, vel_ref, stiff_ref, mass_ref, table_v, table_s,
                u, v, kst, gath, edge, halo, far_table_v, far_table_s, flat, cur, own_a, own_b, acc, fint,
                zsend, psend, rsend, recv, hsend, hrecv, tsend, trecv, tlocal):
    depth, rows, width = stiff_ref.shape
    devices = count_gx * count_gy
    bits = count_gy.bit_length() - 1
    half = count_gy // 2
    fields = 4 * depth
    tall = -(-fields // 8) * 8
    gx = lax.axis_index("gx")
    gy = lax.axis_index("gy")
    me = gx * count_gy + gy
    order = [(k, m) for total in range(count_gx + half - 1) for m in range(half)
             for k in [total - m] if 0 <= k < count_gx]
    flips = [(1 - 2 * ((gy // (1 << k)) % 2)) * (1 << k) for k in range(bits)]
    side = gy % 2
    middle = list(range(1, bits))
    steps = [side * flips[b] + (1 - side) * flips[a] for a, b in zip(middle, middle[::-1])]
    steps.append(flips[0])

    def spot(j):
        k = jnp.int32(0)
        m = jnp.int32(0)
        for i, (a, b) in enumerate(order):
            if a:
                k = k + jnp.where(j == i, a, 0)
            if b:
                m = m + jnp.where(j == i, b, 0)
        return k, m

    def own_slot(k, m):
        column = gy
        for b in range(bits - 1):
            column = column + (m // (1 << b)) % 2 * steps[b]
        return lax.rem(gx + k, count_gx) * count_gy + column

    def partner_slot(k, m):
        column = gy + flips[0]
        for b in range(bits - 1):
            column = column + (m // (1 << b)) % 2 * steps[bits - 2 - b]
        return lax.rem(gx + k, count_gx) * count_gy + column

    def peer_of(p):
        return (p // count_gy, lax.rem(p, count_gy))

    barrier = pltpu.get_barrier_semaphore()

    @pl.loop(1, devices)
    def _(k):
        pl.semaphore_signal(barrier, inc=1, device_id=peer_of(lax.rem(me + k, devices)), device_id_type=MESH)

    lane = lax.broadcasted_iota(i32, (rows, width), 1)
    sub = lax.broadcasted_iota(i32, (rows, width), 0)
    lane_t = lax.broadcasted_iota(i32, (tall, width), 1)
    sub_t = lax.broadcasted_iota(i32, (tall, width), 0)
    lane1 = lax.broadcasted_iota(i32, (1, width), 1)
    row8 = lax.broadcasted_iota(i32, (8, width), 0)
    scale = math.sqrt(math.log2(math.e) / kernel_width)
    stiff_coef = penalty / (8.0 * width)
    damp_coef = damping / (8.0 * width)
    place = (lane.astype(f32) - (width - 1) / 2.0) * (frame_extent / width)
    inside = (sub + gx * rows < rows * count_gx - 1) & (lane + gy * width < width * count_gy - 1)

    u[...] = disp_ref[...]
    v[...] = vel_ref[...]
    for z in range(depth):
        kst[z] = jnp.where(inside, stiff_ref[z], 0.0) if z < depth - 1 else jnp.zeros((rows, width), f32)
    flat[pl.ds(4, rows, stride=8), :] = jnp.ones((rows, width), f32)

    around = [(dx, dy) for dx in (-1, 0, 1) for dy in (-1, 0, 1) if (dx, dy) != (0, 0)]
    base_of = {}
    size_of = {}
    start = 0
    for dx, dy in around:
        base_of[dx, dy] = start
        size_of[dx, dy] = rows if dx == 0 else (tall + 8 if dy == 0 else 8)
        start += size_of[dx, dy]

    def halo_copy(step, n):
        dx, dy = around[n]
        if dx == 0:
            first = tall
        elif dy == 0:
            first = 0 if dx < 0 else tall + rows - 8
        else:
            first = tall if dx < 0 else tall + rows - 8
        peer = (lax.rem(gx + dx + count_gx, count_gx), lax.rem(gy + dy + count_gy, count_gy))
        return pltpu.make_async_remote_copy(
            src_ref=edge.at[step, pl.ds(first, size_of[dx, dy])],
            dst_ref=halo.at[step, pl.ds(base_of[-dx, -dy], size_of[dx, dy])],
            send_sem=hsend.at[n],
            recv_sem=hrecv.at[step, n],
            device_id=peer,
            device_id_type=MESH,
        )

    def slot_copy(step, slot, peer, sem):
        return pltpu.make_async_remote_copy(
            src_ref=gath.at[step, slot],
            dst_ref=gath.at[step, slot],
            send_sem=sem,
            recv_sem=recv.at[step, slot],
            device_id=peer,
            device_id_type=MESH,
        )

    def table_copy(k):
        p = lax.rem(me + k, devices)
        return pltpu.make_async_remote_copy(
            src_ref=table_v.at[p],
            dst_ref=far_table_v.at[me],
            send_sem=tsend.at[k],
            recv_sem=trecv.at[me],
            device_id=peer_of(p),
            device_id_type=MESH,
        )

    def field(j):
        f, z = divmod(j, depth)
        return u[f, z] if f < 3 else kst[z]

    def slot_tiles(step, slot):
        n = None
        for c in range(3):
            s = gath[step, slot, c * rows : (c + 1) * rows]
            n = s * s if n is None else n + s * s
            flat[pl.ds(c, rows, stride=8), :] = s
            flat[pl.ds(5 + c, rows, stride=8), :] = gath[step, slot, (3 + c) * rows : (4 + c) * rows]
        flat[pl.ds(3, rows, stride=8), :] = -n
        cur[...] = flat[...].reshape(rows, 8, width)

    group_lane = lax.broadcasted_iota(i32, (width, 16 * capacity), 1) // 8
    one_lane = lax.broadcasted_iota(i32, (8, 8 * rows), 1)
    one_row = lax.broadcasted_iota(i32, (8, 8 * rows), 0) * rows
    blank = jnp.zeros((48, width), bf16)

    def slot_pairs(slot):
        pairs = []
        for p in range(capacity):
            t = table_s[slot, 0, p]
            pairs.append((lax.shift_right_logical(t, 8), t & (PACK - 1)))
            t = far_table_s[slot, 0, p]
            pairs.append((t & (PACK - 1), lax.shift_right_logical(t, 8)))
        fars = []
        pulls = []
        spots = []
        for r, b in pairs:
            x = cur[b]
            a, bq, c = split3(x)
            first = jnp.concatenate([a, bq], axis=0).astype(bf16)
            second = jnp.concatenate([c, a], axis=0).astype(bf16)
            fars.append(jnp.concatenate([first, first, second], axis=0))
            pulls.append(jnp.where(row8 >= 4, a, pltpu.roll(bq, 4, 0)))
            spots.append(jnp.where(one_lane == r + one_row, 1.0, 0.0))
        weights = []
        for h in range(capacity):
            far = jnp.concatenate([jnp.concatenate([fars[2 * h], blank], axis=1),
                                   jnp.concatenate([blank, fars[2 * h + 1]], axis=1)], axis=0)
            o = own_a[pairs[2 * h][0]] + own_b[pairs[2 * h + 1][0]]
            e = jnp.dot(o, far, preferred_element_type=f32)
            weights.append(jnp.exp2(e).astype(bf16))
        w = jnp.concatenate(weights, axis=1)
        pull = jnp.concatenate(pulls, axis=0).T.astype(bf16)
        rhs = jnp.concatenate([jnp.where(group_lane == p, pull, jnp.zeros_like(pull)) for p in range(2 * capacity)], axis=0)
        t = jnp.dot(w, rhs, preferred_element_type=f32)
        hi = t.astype(bf16)
        lo = (t - hi.astype(f32)).astype(bf16)
        s = jnp.concatenate(spots, axis=0).astype(bf16)
        return jnp.dot(hi, s, preferred_element_type=f32) + jnp.dot(lo, s, preferred_element_type=f32)

    def internal(step):
        def piece(dx, dy, first, size):
            return halo[step, pl.ds(base_of[dx, dy] + first, size), :]

        def down(x, last):
            return jnp.where(sub == rows - 1, last, pltpu.roll(x, rows - 1, 0))

        left = pltpu.roll(piece(0, -1, 0, rows), width // 2, 1)
        right = piece(0, 1, 0, rows)
        own_col = edge[step, pl.ds(tall, rows), :]
        top = piece(-1, 0, 8, tall)
        top_col = piece(-1, 0, 0, 8)[7:8]
        bottom = piece(1, 0, 0, tall)
        bottom_col = piece(1, 0, tall, 8)[0:1]
        top_left = pltpu.roll(piece(-1, -1, 0, 8), width // 2, 1)[7:8]
        top_right = piece(-1, 1, 0, 8)[7:8]
        bottom_left = pltpu.roll(piece(1, -1, 0, 8), width // 2, 1)[0:1]
        bottom_right = piece(1, 1, 0, 8)[0:1]
        own_row = edge[step, pl.ds(0, tall), :]

        right_sum = right + down(right, bottom_right)

        def column(sums, ks, lanes):
            zs = sums + pltpu.roll(sums, width - 1, 1)
            k = ks
            for f in range(3):
                k = jnp.where((lanes >= f * depth) & (lanes < (f + 1) * depth), pltpu.roll(ks, width - (3 - f) * depth, 1), k)
            g = jnp.where(lanes < 3 * depth, k * 0.125 * zs, jnp.where(lanes < fields, ks, 0.0))
            return g + pltpu.roll(g, 1, 1)

        col = left + own_col
        col_sum = col + down(col, bottom_left + bottom_col)
        col_part = column(col_sum, left, lane)
        corner8 = jnp.broadcast_to(top_left + top_col + col[0:1], (8, width))
        corner_k = jnp.broadcast_to(top_left, (8, width))
        corner = column(corner8, corner_k, lax.broadcasted_iota(i32, (8, width), 1))
        col_part = col_part + jnp.where(sub == 0, corner[0:1], pltpu.roll(col_part, 1, 0))

        row_sum = top + own_row
        end = jnp.broadcast_to(top_right + right[0:1], (tall, width))
        end = jnp.sum(jnp.where(lane_t == sub_t, end, 0.0), axis=1, keepdims=True)
        row_sum = row_sum + jnp.where(lane_t == width - 1, end, pltpu.roll(row_sum, width - 1, 1))
        row_sum = row_sum + pltpu.roll(row_sum, tall - 1, 0)
        k = top
        for f in range(3):
            k = jnp.where((sub_t >= f * depth) & (sub_t < (f + 1) * depth), pltpu.roll(top, tall - (3 - f) * depth, 0), k)
        g = jnp.where(sub_t < 3 * depth, k * 0.125 * row_sum, jnp.where(sub_t < fields, top, 0.0))
        g = g + pltpu.roll(g, 1, 0)
        row_part = g + jnp.where(lane_t == 0, 0.0, pltpu.roll(g, 1, 1))

        def spread(x, j):
            x = x + jnp.where(sub == 0, 0.0, pltpu.roll(x, 1, 0))
            x = x + jnp.where(lane == 0, 0.0, pltpu.roll(x, 1, 1))
            side_col = col_part if j == 0 else pltpu.roll(col_part, width - j, 1)
            x = x + jnp.where(lane == 0, side_col, 0.0)
            return x + jnp.where(sub == 0, row_part[j : j + 1], 0.0)

        ks = [kst[z] for z in range(depth - 1)]
        total_k = []
        for z in range(depth):
            x = ks[0] if z == 0 else (ks[z - 1] if z == depth - 1 else ks[z] + ks[z - 1])
            total_k.append(spread(x, 3 * depth + z))
        for f in range(3):
            flat = []
            for z in range(depth):
                j = f * depth + z
                x = u[f, z]
                x = x + down(x, bottom[j : j + 1])
                x = x + jnp.where(lane == width - 1, pltpu.roll(right_sum, width - 1 - j, 1), pltpu.roll(x, width - 1, 1))
                flat.append(x)
            g = [ks[z] * 0.125 * (flat[z] + flat[z + 1]) for z in range(depth - 1)]
            for z in range(depth):
                x = g[0] if z == 0 else (g[z - 1] if z == depth - 1 else g[z] + g[z - 1])
                fint[f, z] = spread(x, f * depth + z) - u[f, z] * total_k[z]

    def relay(step, j):
        k, m = spot(j)
        slot = own_slot(k, m)
        slot_copy(step, slot, peer_of(lax.rem(me + 1, devices)), psend.at[0]).wait_recv()
        for b in range(bits):
            @pl.when(m < (1 << b))
            def _(b=b):
                slot_copy(step, slot, (gx, gy + steps[b]), rsend.at[j, b]).start()

    @pl.loop(0, STEPS)
    def _(step):
        for c in range(3):
            p = u[c, depth - 1]
            if c == 1:
                p = p + place
            gath[step, me, c * rows : (c + 1) * rows] = scale * p
            gath[step, me, (3 + c) * rows : (4 + c) * rows] = stiff_coef * p - damp_coef * v[c, depth - 1]
        col = jnp.zeros((rows, width), f32)
        for j in range(fields):
            x = field(j)
            col = jnp.where(lane == j, x if j == 0 else pltpu.roll(x, j, 1), col)
            col = jnp.where(lane == width // 2 + j, pltpu.roll(x, width // 2 + 1 + j, 1), col)
            edge[step, j : j + 1] = x[0:1]
            edge[step, tall + rows + j : tall + rows + j + 1] = x[rows - 1 : rows]
        edge[step, tall : tall + rows] = col
        if tall > fields:
            edge[step, fields:tall] = jnp.zeros((tall - fields, width), f32)
            edge[step, tall + rows + fields :] = jnp.zeros((tall - fields, width), f32)

        @pl.when(step == 0)
        def _():
            pl.semaphore_wait(barrier, devices - 1)

        for k in range(1, count_gx):
            slot_copy(step, me, (lax.rem(gx + k, count_gx), gy), zsend.at[k]).start()
        for b in range(bits):
            slot_copy(step, me, (gx, gy + steps[b]), psend.at[b]).start()
        for n in range(len(around)):
            halo_copy(step, n).start()

        @pl.when(step == 0)
        def _():
            @pl.loop(1, devices)
            def _(k):
                table_copy(k).start()

        slot_tiles(step, me)

        @pl.loop(0, rows, unroll=4)
        def _(r):
            x = cur[r]
            norm = jnp.broadcast_to(x[3:4], x.shape)
            y = jnp.where(row8 < 3, 2.0 * x, jnp.where(row8 == 3, 1.0, jnp.where(row8 == 4, norm, 0.0)))
            a, b, c = split3(y)
            pack = jnp.concatenate([a, a, b, b, a, c], axis=0)
            zero = jnp.zeros_like(pack)
            own_a[r] = jnp.concatenate([pack, zero], axis=0).T.astype(bf16)
            own_b[r] = jnp.concatenate([zero, pack], axis=0).T.astype(bf16)

        @pl.loop(1, 1 + AHEAD)
        def _(j):
            relay(step, j)

        acc[...] = jnp.zeros_like(acc)

        for n in range(len(around)):
            halo_copy(step, n).wait_recv()
        internal(step)

        @pl.when(step == 0)
        def _():
            far_table_v[me] = table_v[me]

            @pl.loop(1, devices)
            def _(k):
                q = lax.rem(me + k, devices)
                pltpu.make_async_remote_copy(
                    src_ref=table_v.at[q], dst_ref=far_table_v.at[q], send_sem=tsend.at[k], recv_sem=trecv.at[q],
                    device_id=peer_of(q), device_id_type=MESH,
                ).wait_recv()
            keep = pltpu.make_async_copy(far_table_v, far_table_s, tlocal)
            keep.start()
            keep.wait()

        waves = len(order)

        @pl.loop(1, waves + 1)
        def _(j):
            @pl.when(j + AHEAD < waves)
            def _():
                relay(step, j + AHEAD)
            k, m = spot(j)
            slot = own_slot(k, m)
            slot_tiles(step, slot)
            one = slot_pairs(slot)
            k, m = spot(j - 1)
            slot = partner_slot(k, m)
            slot_copy(step, slot, peer_of(lax.rem(me + 1, devices)), psend.at[0]).wait_recv()
            slot_tiles(step, slot)
            acc[...] += one + slot_pairs(slot)

        total = acc[...]
        pieces = [total[:, i * width : (i + 1) * width].T for i in range(8 * rows // width)]
        total = pieces[0] if len(pieces) == 1 else jnp.concatenate(pieces, axis=0)
        count = total[4 * rows : 5 * rows]
        for c in range(3):
            q = gath[step, me, (3 + c) * rows : (4 + c) * rows]
            pulled = total[(5 + c) * rows : (6 + c) * rows] + total[(1 + c) * rows : (2 + c) * rows]
            fint[c, depth - 1] = fint[c, depth - 1] + q * count - pulled
        for z in range(depth):
            rate = time_step * mass_ref[z]
            for c in range(3):
                speed = v[c, z] + rate * fint[c, z]
                v[c, z] = speed
                u[c, z] = u[c, z] + time_step * speed

        for k in range(1, count_gx):
            slot_copy(step, me, (lax.rem(gx + k, count_gx), gy), zsend.at[k]).wait_send()
        for b in range(bits):
            slot_copy(step, me, (gx, gy + steps[b]), psend.at[b]).wait_send()
        for n in range(len(around)):
            halo_copy(step, n).wait_send()

        @pl.loop(1, waves)
        def _(j):
            k, m = spot(j)
            slot = own_slot(k, m)
            for b in range(bits):
                @pl.when(m < (1 << b))
                def _(b=b):
                    slot_copy(step, slot, (gx, gy + steps[b]), rsend.at[j, b]).wait_send()

        @pl.when(step == 0)
        def _():
            @pl.loop(1, devices)
            def _(k):
                table_copy(k).wait_send()


def local(displacement, velocity, stiffness, inverse_mass, facing):
    count_gx = lax.axis_size("gx")
    count_gy = lax.axis_size("gy")
    devices = count_gx * count_gy
    rows, depth, width = stiffness.shape
    per_row = facing.shape[2]
    requests = per_row * rows
    capacity = requests // devices
    bits = count_gy.bit_length() - 1
    waves = devices // 2
    fields = 4 * depth
    tall = -(-fields // 8) * 8
    vmem = pl.BlockSpec(memory_space=pltpu.VMEM)
    smem = pl.BlockSpec(memory_space=pltpu.SMEM)
    table = pl.pallas_call(
        functools.partial(table_kernel, count_gy, capacity, per_row, rows),
        out_shape=jax.ShapeDtypeStruct((devices, 1, 128), i32),
        in_specs=[vmem],
        out_specs=vmem,
        name="tables",
    )(facing.reshape(1, requests))
    whole = (3, depth, rows, width)
    dma = pltpu.SemaphoreType.DMA
    u, v = pl.pallas_call(
        functools.partial(step_kernel, count_gx, count_gy, capacity),
        out_shape=(jax.ShapeDtypeStruct(whole, f32), jax.ShapeDtypeStruct(whole, f32)),
        in_specs=[vmem] * 5 + [smem],
        out_specs=(vmem, vmem),
        scratch_shapes=[
            pltpu.VMEM((depth, rows, width), f32),
            pltpu.VMEM((STEPS, devices, 6 * rows, width), f32),
            pltpu.VMEM((STEPS, 2 * tall + rows, width), f32),
            pltpu.VMEM((STEPS, 2 * rows + 2 * (tall + 8) + 32, width), f32),
            pltpu.VMEM((devices, 1, 128), i32),
            pltpu.SMEM((devices, 1, 128), i32),
            pltpu.VMEM((8 * rows, width), f32),
            pltpu.VMEM((rows, 8, width), f32),
            pltpu.VMEM((rows, width, 96), bf16),
            pltpu.VMEM((rows, width, 96), bf16),
            pltpu.VMEM((width, 8 * rows), f32),
            pltpu.VMEM(whole, f32),
            dma((count_gx,)),
            dma((bits,)),
            dma((waves, bits)),
            dma((STEPS, devices)),
            dma((8,)),
            dma((STEPS, 8)),
            dma((devices,)),
            dma((devices,)),
            dma,
        ],
        compiler_params=pltpu.CompilerParams(collective_id=0, has_side_effects=True),
        name="steps",
    )(
        displacement.transpose(0, 2, 1, 3),
        velocity.transpose(0, 2, 1, 3),
        stiffness.transpose(1, 0, 2),
        inverse_mass.transpose(1, 0, 2),
        table,
        table,
    )
    return u.transpose(0, 2, 1, 3), v.transpose(0, 2, 1, 3)


def solution(mesh):
    in_specs = (
        P(None, "gx", None, "gy"),
        P(None, "gx", None, "gy"),
        P("gx", None, "gy"),
        P("gx", None, "gy"),
        P("gx", "gy", None),
    )
    out_specs = (P(None, "gx", None, "gy"), P(None, "gx", None, "gy"))
    return jax.shard_map(local, mesh=mesh, in_specs=in_specs, out_specs=out_specs, check_vma=False)
```

time: 153 us -> 84.7 us (0.55)
  Pallas kernels: 111 us -> 80.1 us
  local copies, waits for them, and re-layouts: 24 us -> 3.8 us
  other arithmetic: 15 us -> 0 us
    pallas_call x4 -> x2, Pallas kernels: 111 us -> 80.1 us  [the longest x1 78.4 us: local(): pl.pallas_call(functools.partial(step_kernel, count_gx, count_gy, capacit...]
    slice x39 -> x0, local copies, waits for them, and re-layouts: 9.05 us -> none  [the longest x8 4.23 us: pack_edges(): sides_y = {-1: stacked[:, :, :, 0], 1: stacked[:, :, :, width_y - 1]}]
    reshape x32 -> x1, local copies, waits for them, and re-layouts: 8.34 us -> 0.65 us  [local(): facing.reshape(1, requests)]
    concatenate x7 -> x0, other arithmetic: 4.78 us -> none  [the longest x2 2.75 us: unpack_edges(): return jnp.concatenate(lines, axis=3)]
    add x12 -> x0, other arithmetic: 2.23 us -> none  [the longest x2 0.64 us: local(): displacement = displacement + time_step * velocity]
    reduce_sum x3 -> x0, other arithmetic: 2.09 us -> none  [the longest x1 1.23 us: local(): jnp.sum(jnp.where(pick, source[:, None, :], 0), axis=2).reshape(requests)]
    mul x6 -> x0, other arithmetic: 1.74 us -> none  [the longest x1 0.9 us: local(): velocity = velocity + time_step * inverse_mass[None] * total_force]
    another operation x17 -> x0, local copies, waits for them, and re-layouts: 1.54 us -> none  [the longest x12 1.52 us: pack_edges(): part = part.reshape(-1)]
where the time goes in v1:
time: 84.7 us; the launch traced here: 84.5 us
  Pallas kernels  80.1 us (95%)
  local copies, waits for them, and re-layouts  3.8 us (4%)
    pallas_call x1, Pallas kernels, local(): pl.pallas_call(functools.partial(step_kernel, count_gx, count_gy, capacit...  78.4 us
    unnamed x7, local copies, waits for them, and re-layouts  3.15 us

profile of v1, /device:TPU:8, one launch (start us, length us, event | category | flops | bytes accessed | tf_op | source)
XLA Modules:
  0.0 84.5 jit_solution(5076387771483260593)
XLA Ops:
  0.6 0.0 copy-start.1
  0.6 0.7 copy-done.1
  1.3 0.1 copy.8
  1.4 0.7 reshape.7.wanted_ref
  2.0 1.6 %tables.1.table_v.table_s = s32[32,1,128]{2,1,0:T(1,128)} custom-call(s32[1,256]{1,0:T(1,128)} %reshape.7.wanted_ref), custom_call_target="tpu_custom_call" | custom-call | tf_op jit(solution)/shard_map/tables/pallas_call | solution.py:455
  3.7 78.4 %steps.1 = (f32[3,5,32,128]{3,2,1,0:T(8,128)}, f32[3,5,32,128]{3,2,1,0:T(8,128)}) custom-call(f32[3,5,32,128]{3,2,1,0:T(8,128)} %bitcast.10, f32[3,5,32,128]{3,2,1,0:T(8,128)} %bitcast.11, f32[5,32,128]{2,1,0:T(8,128)} %bitcast.12, f32[5,32,128]{2,1,0:T(8,128)} %bitcast.13, s32[32,1,128]{2,1,0:T(1,128)} %tables.1.table_v.table_s, ...), custom_call_target="tpu_custom_call" | custom-call | tf_op jit(solution)/shard_map/steps/pallas_call | solution.py:464
  82.1 0.0 copy-start
  82.1 1.7 %copy.11 = f32[3,32,5,128]{3,1,2,0:T(8,128)} copy(f32[3,32,5,128]{3,1,2,0:T(8,128)} %bitcast.9) | data formatting | bytes 491520
  83.8 0.0 copy-done
  83.8 0.7 copy.12
Async XLA Ops:
  0.6 0.7 copy-start.1
  82.1 1.7 %copy-start = (f32[3,5,32,128]{3,2,1,0:T(8,128)S(1)}, f32[3,5,32,128]{3,2,1,0:T(8,128)}, u32[]{:S(2)}) copy-start(f32[3,5,32,128]{3,2,1,0:T(8,128)} %get-tuple-element.5) | copy-start | bytes 737284

commit v2 on v1

--- a/solution.py
+++ b/solution.py
@@ -66,8 +66,7 @@
     gx = lax.axis_index("gx")
     gy = lax.axis_index("gy")
     me = gx * count_gy + gy
-    order = [(k, m) for total in range(count_gx + half - 1) for m in range(half)
-             for k in [total - m] if 0 <= k < count_gx]
+    order = sorted(((k, m) for k in range(count_gx) for m in range(half)), key=lambda a: (a[0] + 1.6 * a[1], a[1]))
     flips = [(1 - 2 * ((gy // (1 << k)) % 2)) * (1 << k) for k in range(bits)]
     side = gy % 2
     middle = list(range(1, bits))
@@ -84,17 +83,24 @@
                 m = m + jnp.where(j == i, b, 0)
         return k, m
 
+    room = jnp.minimum(gx, count_gx - 1 - gx)
+    toward = jnp.where(count_gx - 1 - gx > gx, 1, -1)
+
+    def source(k):
+        near = jnp.where(lax.rem(k, 2) == 1, lax.div(k + 1, 2), -lax.div(k, 2))
+        return gx + jnp.where(k <= 2 * room, near, toward * (k - room))
+
     def own_slot(k, m):
         column = gy
         for b in range(bits - 1):
             column = column + (m // (1 << b)) % 2 * steps[b]
-        return lax.rem(gx + k, count_gx) * count_gy + column
+        return source(k) * count_gy + column
 
     def partner_slot(k, m):
         column = gy + flips[0]
         for b in range(bits - 1):
             column = column + (m // (1 << b)) % 2 * steps[bits - 2 - b]
-        return lax.rem(gx + k, count_gx) * count_gy + column
+        return source(k) * count_gy + column
 
     def peer_of(p):
         return (p // count_gy, lax.rem(p, count_gy))
@@ -121,7 +127,8 @@
     v[...] = vel_ref[...]
     for z in range(depth):
         kst[z] = jnp.where(inside, stiff_ref[z], 0.0) if z < depth - 1 else jnp.zeros((rows, width), f32)
-    flat[pl.ds(4, rows, stride=8), :] = jnp.ones((rows, width), f32)
+    for i in range(2):
+        flat[i, pl.ds(4, rows, stride=8), :] = jnp.ones((rows, width), f32)
 
     around = [(dx, dy) for dx in (-1, 0, 1) for dy in (-1, 0, 1) if (dx, dy) != (0, 0)]
     base_of = {}
@@ -175,22 +182,22 @@
         f, z = divmod(j, depth)
         return u[f, z] if f < 3 else kst[z]
 
-    def slot_tiles(step, slot):
+    def slot_tiles(step, slot, i):
         n = None
         for c in range(3):
             s = gath[step, slot, c * rows : (c + 1) * rows]
             n = s * s if n is None else n + s * s
-            flat[pl.ds(c, rows, stride=8), :] = s
-            flat[pl.ds(5 + c, rows, stride=8), :] = gath[step, slot, (3 + c) * rows : (4 + c) * rows]
-        flat[pl.ds(3, rows, stride=8), :] = -n
-        cur[...] = flat[...].reshape(rows, 8, width)
+            flat[i, pl.ds(c, rows, stride=8), :] = s
+            flat[i, pl.ds(5 + c, rows, stride=8), :] = gath[step, slot, (3 + c) * rows : (4 + c) * rows]
+        flat[i, pl.ds(3, rows, stride=8), :] = -n
+        cur[i] = flat[i].reshape(rows, 8, width)
 
     group_lane = lax.broadcasted_iota(i32, (width, 16 * capacity), 1) // 8
     one_lane = lax.broadcasted_iota(i32, (8, 8 * rows), 1)
     one_row = lax.broadcasted_iota(i32, (8, 8 * rows), 0) * rows
     blank = jnp.zeros((48, width), bf16)
 
-    def slot_pairs(slot):
+    def slot_pairs(slot, i):
         pairs = []
         for p in range(capacity):
             t = table_s[slot, 0, p]
@@ -201,7 +208,7 @@
         pulls = []
         spots = []
         for r, b in pairs:
-            x = cur[b]
+            x = cur[i, b]
             a, bq, c = split3(x)
             first = jnp.concatenate([a, bq], axis=0).astype(bf16)
             second = jnp.concatenate([c, a], axis=0).astype(bf16)
@@ -333,7 +340,7 @@
             pl.semaphore_wait(barrier, devices - 1)
 
         for k in range(1, count_gx):
-            slot_copy(step, me, (lax.rem(gx + k, count_gx), gy), zsend.at[k]).start()
+            slot_copy(step, me, (source(jnp.int32(k)), gy), zsend.at[k]).start()
         for b in range(bits):
             slot_copy(step, me, (gx, gy + steps[b]), psend.at[b]).start()
         for n in range(len(around)):
@@ -345,11 +352,10 @@
             def _(k):
                 table_copy(k).start()
 
-        slot_tiles(step, me)
-
-        @pl.loop(0, rows, unroll=4)
-        def _(r):
-            x = cur[r]
+        slot_tiles(step, me, 0)
+
+        def prepare(r):
+            x = cur[0, r]
             norm = jnp.broadcast_to(x[3:4], x.shape)
             y = jnp.where(row8 < 3, 2.0 * x, jnp.where(row8 == 3, 1.0, jnp.where(row8 == 4, norm, 0.0)))
             a, b, c = split3(y)
@@ -358,9 +364,13 @@
             own_a[r] = jnp.concatenate([pack, zero], axis=0).T.astype(bf16)
             own_b[r] = jnp.concatenate([zero, pack], axis=0).T.astype(bf16)
 
+        pl.loop(0, rows // 2, unroll=4)(prepare)
+
         @pl.loop(1, 1 + AHEAD)
         def _(j):
             relay(step, j)
+
+        pl.loop(rows // 2, rows, unroll=4)(prepare)
 
         acc[...] = jnp.zeros_like(acc)
 
@@ -385,20 +395,18 @@
 
         waves = len(order)
 
-        @pl.loop(1, waves + 1)
+        @pl.loop(0, waves)
         def _(j):
-            @pl.when(j + AHEAD < waves)
+            @pl.when((j > 0) & (j + AHEAD < waves))
             def _():
                 relay(step, j + AHEAD)
             k, m = spot(j)
-            slot = own_slot(k, m)
-            slot_tiles(step, slot)
-            one = slot_pairs(slot)
-            k, m = spot(j - 1)
-            slot = partner_slot(k, m)
-            slot_copy(step, slot, peer_of(lax.rem(me + 1, devices)), psend.at[0]).wait_recv()
-            slot_tiles(step, slot)
-            acc[...] += one + slot_pairs(slot)
+            mine = own_slot(k, m)
+            other = partner_slot(k, m)
+            slot_copy(step, other, peer_of(lax.rem(me + 1, devices)), psend.at[0]).wait_recv()
+            slot_tiles(step, mine, 0)
+            slot_tiles(step, other, 1)
+            acc[...] += slot_pairs(mine, 0) + slot_pairs(other, 1)
 
         total = acc[...]
         pieces = [total[:, i * width : (i + 1) * width].T for i in range(8 * rows // width)]
@@ -416,7 +424,7 @@
                 u[c, z] = u[c, z] + time_step * speed
 
         for k in range(1, count_gx):
-            slot_copy(step, me, (lax.rem(gx + k, count_gx), gy), zsend.at[k]).wait_send()
+            slot_copy(step, me, (source(jnp.int32(k)), gy), zsend.at[k]).wait_send()
         for b in range(bits):
             slot_copy(step, me, (gx, gy + steps[b]), psend.at[b]).wait_send()
         for n in range(len(around)):
@@ -473,8 +481,8 @@
             pltpu.VMEM((STEPS, 2 * rows + 2 * (tall + 8) + 32, width), f32),
             pltpu.VMEM((devices, 1, 128), i32),
             pltpu.SMEM((devices, 1, 128), i32),
-            pltpu.VMEM((8 * rows, width), f32),
-            pltpu.VMEM((rows, 8, width), f32),
+            pltpu.VMEM((2, 8 * rows, width), f32),
+            pltpu.VMEM((2, rows, 8, width), f32),
             pltpu.VMEM((rows, width, 96), bf16),
             pltpu.VMEM((rows, width, 96), bf16),
             pltpu.VMEM((width, 8 * rows), f32),

time: 84.7 us -> 80 us (0.945)
  Pallas kernels: 80.1 us -> 75.2 us
    pallas_call x1, Pallas kernels: 78.4 us -> 73.6 us  [local(): pl.pallas_call(functools.partial(step_kernel, count_gx, count_gy, capacit...]
where the time goes in v2:
time: 80 us; the launch traced here: 79.7 us
  Pallas kernels  75.2 us (94%)
  local copies, waits for them, and re-layouts  3.8 us (5%)
    pallas_call x1, Pallas kernels, local(): pl.pallas_call(functools.partial(step_kernel, count_gx, count_gy, capacit...  73.6 us
    unnamed x7, local copies, waits for them, and re-layouts  3.15 us
    pallas_call x1, Pallas kernels, local(): pl.pallas_call(functools.partial(table_kernel, count_gy, capacity, per_ro...  1.63 us

profile of v2, /device:TPU:8, one launch (start us, length us, event | category | flops | bytes accessed | tf_op | source)
XLA Modules:
  0.0 79.7 jit_solution(10403007655336477207)
XLA Ops:
  0.6 0.0 copy-start.1
  0.6 0.7 copy-done.1
  1.3 0.1 copy.8
  1.4 0.7 reshape.7.wanted_ref
  2.0 1.6 %tables.1.table_v.table_s = s32[32,1,128]{2,1,0:T(1,128)} custom-call(s32[1,256]{1,0:T(1,128)} %reshape.7.wanted_ref), custom_call_target="tpu_custom_call" | custom-call | tf_op jit(solution)/shard_map/tables/pallas_call | solution.py:463
  3.7 73.6 %steps.1 = (f32[3,5,32,128]{3,2,1,0:T(8,128)}, f32[3,5,32,128]{3,2,1,0:T(8,128)}) custom-call(f32[3,5,32,128]{3,2,1,0:T(8,128)} %bitcast.10, f32[3,5,32,128]{3,2,1,0:T(8,128)} %bitcast.11, f32[5,32,128]{2,1,0:T(8,128)} %bitcast.12, f32[5,32,128]{2,1,0:T(8,128)} %bitcast.13, s32[32,1,128]{2,1,0:T(1,128)} %tables.1.table_v.table_s, ...), custom_call_target="tpu_custom_call" | custom-call | tf_op jit(solution)/shard_map/steps/pallas_call | solution.py:472
  77.3 0.0 copy-start
  77.3 1.7 %copy.11 = f32[3,32,5,128]{3,1,2,0:T(8,128)} copy(f32[3,32,5,128]{3,1,2,0:T(8,128)} %bitcast.9) | data formatting | bytes 491520
  79.0 0.0 copy-done
  79.0 0.7 copy.12
Async XLA Ops:
  0.6 0.7 copy-start.1
  77.3 1.7 %copy-start = (f32[3,5,32,128]{3,2,1,0:T(8,128)S(1)}, f32[3,5,32,128]{3,2,1,0:T(8,128)}, u32[]{:S(2)}) copy-start(f32[3,5,32,128]{3,2,1,0:T(8,128)} %get-tuple-element.5) | copy-start | bytes 737284
